TPU v7x, 128 devices: a whole 4x4x4 slice. The times are simulated.
128 devices in a mesh: blk: 16 (over y, x), tp: 8 (over z, core).
Axes of the slice: x: 4, y: 4, z: 4, core: 2. Of those that a mesh axis runs over, the one named last changes fastest.
Arguments:
- hidden_in: bfloat16 [8192, 6144], P('blk', 'tp'), may hold values from -40 to 40
- ln_gain: float32 [6144], replicated, may hold values from 0.1 to 1.9
- w_qkv: bfloat16 [6144, 3, 3072], P(None, None, 'tp'), may hold values from -1 to 1
- w_out: bfloat16 [3072, 6144], P('tp'), may hold values from -0.625 to 0.625
- doc_lengths: int32 [64], replicated, may hold values from 0 to 4096, as said below
- segment_ids: int32 [8192], P('blk'), may hold values from 0 to 63, as said below
- pair_table: int32 [16, 16], replicated, may hold values from 0 to 1, as said below
- page_table: int32 [512], P('blk'), may hold values from 0 to 511, as said below
Outputs:
- attn_out: bfloat16 [8192, 6144], P('blk', 'tp')
- page_cache: bfloat16 [2, 512, 16, 3072], P(None, 'blk', None, 'tp')
Inputs may be any that keep to these rules, and one draw needn't show every extreme that they name: `doc_lengths`: the 64 documents in stream order; they sum to 8192, the empty ones stand just before the last slot, which holds the stream's last document, and the second document has exactly 4096 tokens. segment_ids[t] is the number of documents that end at or before token t; the last token belongs to slot 63. pair_table[i, j] is 1 exactly where a token of block j of 512 tokens and a token at or after it in block i lie in one document. `page_table`: the 32 entries of one block of tokens are that block's own page numbers, each once.
All inputs are finite; a program needn't handle non-finite values.
Results may differ from a plain program's by a relative error of at most 0.014.
Values may be sent and summed in bfloat16 or wider, within the bound.
A program may use at most 256 MiB of HBM per device.

v0:
```python
import jax
import jax.numpy as jnp
from jax import lax
from jax.sharding import PartitionSpec as P

HD = 96
ROT = 24
PAGE = 16
EPSILON = 1e-05


def layer_norm(whole, ln_gain):
    values32 = whole.astype(jnp.float32)
    row_mean = jnp.mean(values32, axis=-1, keepdims=True)
    centred = values32 - row_mean
    row_var = jnp.mean(centred * centred, axis=-1, keepdims=True)
    return (centred * lax.rsqrt(row_var + EPSILON) * ln_gain).astype(jnp.bfloat16)


def doc_positions(token_index, doc_lengths, segment_ids):
    starts = jnp.cumsum(doc_lengths) - doc_lengths
    slots = jnp.arange(doc_lengths.shape[0], dtype=jnp.int32)
    in_document = segment_ids[:, None] == slots[None, :]
    offsets = jnp.sum(jnp.where(in_document, starts[None, :], 0), axis=1)
    return token_index - offsets


def rotary(head_block, positions):
    half_rot = ROT // 2
    frequency = 10000.0 ** (-(2.0 * jnp.arange(half_rot, dtype=jnp.float32)) / ROT)
    angles = positions.astype(jnp.float32)[:, None] * frequency[None, :]
    cosine = jnp.cos(angles)[:, None, :]
    sine_part = jnp.sin(angles)[:, None, :]
    lower_half = head_block[..., :half_rot]
    upper_half = head_block[..., half_rot:ROT]
    return jnp.concatenate(
        [
            lower_half * cosine - upper_half * sine_part,
            upper_half * cosine + lower_half * sine_part,
            head_block[..., ROT:],
        ],
        axis=-1,
    )


def per_device(hidden_in, ln_gain, w_qkv, w_out, doc_lengths, segment_ids, pair_table, page_table):
    row_count = hidden_in.shape[0]
    whole = lax.all_gather(hidden_in, "tp", axis=1, tiled=True)
    normed = layer_norm(whole, ln_gain)
    width = whole.shape[1]
    col_count = w_qkv.shape[2]
    head_count = col_count // HD
    projected = jnp.dot(
        normed, w_qkv.reshape(width, 3 * col_count), preferred_element_type=jnp.float32
    ).reshape(row_count, 3, head_count, HD)
    block_index = lax.axis_index("blk")
    token_index = block_index * row_count + jnp.arange(row_count, dtype=jnp.int32)
    positions = doc_positions(token_index, doc_lengths, segment_ids)
    queries = rotary(projected[:, 0], positions).astype(jnp.bfloat16)
    key_rows = rotary(projected[:, 1], positions).astype(jnp.bfloat16)
    values = projected[:, 2].astype(jnp.bfloat16)
    table_row = lax.dynamic_index_in_dim(pair_table, block_index, 0, keepdims=False)
    block_ids = jnp.arange(pair_table.shape[1], dtype=jnp.int32)
    scale = HD ** (-0.5)
    start_state = (
        jnp.full((head_count, row_count), -1e30, jnp.float32),
        jnp.zeros((head_count, row_count), jnp.float32),
        jnp.zeros((head_count, row_count, HD), jnp.float32),
    )
    key_piece = lax.all_gather(key_rows, "blk", axis=0, tiled=True)
    value_piece = lax.all_gather(values, "blk", axis=0, tiled=True)
    segment_piece = lax.all_gather(segment_ids, "blk", axis=0, tiled=True)
    piece_rows = key_piece.shape[0]
    key_index = jnp.arange(piece_rows, dtype=jnp.int32)
    matches = (key_index // row_count)[:, None] == block_ids[None, :]
    live = jnp.sum(jnp.where(matches, table_row[None, :], 0), axis=1) > 0

    def compute(previous):
        maxima, totals, weighted = previous
        scores = (
            jnp.einsum("qhd,khd->hqk", queries, key_piece, preferred_element_type=jnp.float32)
            * scale
        )
        allowed = (
            live[None, :]
            & (segment_ids[:, None] == segment_piece[None, :])
            & (key_index[None, :] <= token_index[:, None])
        )
        scores = jnp.where(allowed[None], scores, -jnp.inf)
        newest = jnp.maximum(maxima, jnp.max(scores, axis=-1))
        weights = jnp.exp(scores - newest[..., None])
        totals = jnp.sum(weights, axis=-1)
        weighted = jnp.einsum(
            "hqk,khd->hqd",
            weights.astype(jnp.bfloat16),
            value_piece,
            preferred_element_type=jnp.float32,
        )
        return (newest, totals, weighted)

    final = lax.cond(jnp.any(live), compute, lambda previous: previous, start_state)
    mixed = (final[2] / final[1][..., None]).astype(jnp.bfloat16)
    heads_out = jnp.transpose(mixed, (1, 0, 2)).reshape(row_count, col_count)
    partial_term = jnp.dot(heads_out, w_out, preferred_element_type=jnp.float32)
    attn_out = lax.psum_scatter(
        partial_term.astype(jnp.bfloat16), "tp", scatter_dimension=1, tiled=True
    )
    page_count = row_count // PAGE
    local_pages = page_table - block_index * page_count
    stacked = jnp.stack(
        [key_rows.reshape(page_count, PAGE, col_count), values.reshape(page_count, PAGE, col_count)]
    )
    page_cache = jnp.zeros_like(stacked).at[:, local_pages].set(stacked)
    return (attn_out, page_cache)


def solution(mesh):
    placed = (P("blk", "tp"), P(), P(None, None, "tp"), P("tp", None), P(), P("blk"), P(), P("blk"))
    return jax.shard_map(
        per_device,
        mesh=mesh,
        in_specs=placed,
        out_specs=(P("blk", "tp"), P(None, "blk", None, "tp")),
        check_vma=False,
    )
```

profile of v0, /device:TPU:1, one launch (start us, length us, event | category | flops | bytes accessed | tf_op | source)
XLA Modules:
  0.0 351.7 jit_solution(17223538342270474863)
XLA Ops:
  7.2 0.7 all-gather.6.cloned.1.call-update
  8.0 18.8 %copy.23 = bf16[6144,3,384]{0,2,1:T(8,128)(2,1)} copy(bf16[6144,3,384]{2,0,1:T(8,128)(2,1)} %param.12) | data formatting | bytes 28311552 | tf_op args[2]
  27.4 26.9 %all-gather.6.cloned.1.call-done = bf16[512,6144]{1,0:T(8,128)(2,1)} async-done(((bf16[512,768]{1,0:T(8,128)(2,1)}), bf16[512,6144]{1,0:T(8,128)(2,1)}) %all-gather.6.cloned.1.call-update) | async-done | bytes 6291472 | tf_op jit(solution)/shard_map/all_gather | solution.py:48
  54.4 3.8 %convert_reduce_fusion = f32[512]{0:T(512)S(1)} fusion(bf16[512,6144]{1,0:T(8,128)(2,1)} %all-gather.6.cloned.1.call-done), kind=kLoop, calls=%fused_computation.14 | loop fusion | flops 6290944 | bytes 6293504 | tf_op jit(solution)/shard_map/reduce_sum | solution.py:14
  58.2 4.6 %fusion.10 = f32[512]{0:T(512)S(1)} fusion(bf16[512,6144]{1,0:T(8,128)(2,1)} %all-gather.6.cloned.1.call-done, f32[512]{0:T(512)S(1)} %broadcast_multiply_fusion), kind=kLoop, calls=%fused_computation.17 | loop fusion | flops 12582400 | bytes 6295552 | tf_op jit(solution)/shard_map/reduce_sum | solution.py:16
  62.8 11.8 %fusion.14 = f32[512,3,4,96]{0,3,2,1:T(8,128)S(1)} fusion(bf16[3,4,96,6144]{3,2,1,0:T(8,128)(2,1)} %bitcast.33, bf16[512,6144]{1,0:T(8,128)(2,1)S(1)} %copy-done.2, f32[6144]{0:T(1024)S(1)} %copy-done.8, f32[512]{0:T(512)S(1)} %add_rsqrt_fusion, f32[512]{0:T(512)S(1)} %broadcast_multiply_fusion), kind=kOutput, calls=%fused_computation.22 | convolution fusion | flops 7263485952 | bytes 22835200 | tf_op jit(solution)/shard_map/dot_general | solution.py:53
  74.9 0.8 maximum_convert_fusion
  75.8 0.8 slice.58
  76.9 0.6 fusion.22
  78.2 19.2 %all-gather.1 = s32[16,1,512]{2,1,0:T(1,128)S(1)} all-gather(s32[1,1,512]{2,1,0:T(1,128)S(1)} %bitcast.36), channel_id=1, replica_groups=mesh['blk'=16,'tp'=8] {'blk'}, dimensions={0}, use_global_device_ids=true | all-gather | bytes 34816 | tf_op jit(solution)/shard_map/all_gather | solution.py:72
  97.5 43.4 %all-gather.8.cloned.1.call-done = bf16[8192,4,96]{0,2,1:T(8,128)(2,1)} async-done(((bf16[512,4,96]{0,2,1:T(8,128)(2,1)}), bf16[8192,4,96]{0,2,1:T(8,128)(2,1)}) %all-gather.8.cloned.1.call-update) | async-done | bytes 6291472 | tf_op jit(solution)/shard_map/all_gather | solution.py:70
  140.9 68.3 %all-gather.10.cloned.1.call-done = bf16[8192,1,4,96]{0,3,2,1:T(8,128)(2,1)} async-done(((bf16[512,1,4,96]{0,3,2,1:T(8,128)(2,1)}), bf16[8192,1,4,96]{0,3,2,1:T(8,128)(2,1)}) %all-gather.10.cloned.1.call-update) | async-done | bytes 6291472 | tf_op jit(solution)/shard_map/all_gather | solution.py:71
  209.2 85.0 %conditional.1 = (f32[4,512]{1,0:T(4,128)S(1)}, f32[4,512,96]{1,2,0:T(8,128)S(1)}) conditional(s32[]{:T(128)} %convert_element_type.56, () %tuple.16, (pred[8192]{0:T(1024)(128)(4,1)S(1)}, s32[512]{0:T(512)S(1)}, s32[8192]{0:T(1024)S(1)}, s32[8192]{0:T(1024)S(1)}, s32[]{:T(128)}, /*index=5*/s32[512]{0:T(512)S(1)}, bf16[512,4,96]{0,2,1:T(8,128)(2,1)S(1)}, ...), branch_computations={%region_6.7_spmd, %region_7.10_spmd} | conditional | flops 6643776000 | bytes 231997456 | solution.py:101
  209.2 5.8 %compare_and_fusion = pred[512,8192]{1,0:T(8,128)(4,1)} fusion(s32[8192]{0:T(1024)S(1)} %get-tuple-element.23, s32[8192]{0:T(1024)S(1)} %get-tuple-element.22, s32[512]{0:T(512)S(1)} %broadcast_add_fusion, s32[512]{0:T(512)S(1)} %get-tuple-element.21, pred[8192]{0:T(1024)(128)(4,1)S(1)} %get-tuple-element.20), kind=kLoop, calls=%fused_computation.8 | loop fusion | flops 16777216 | bytes 4272128 | tf_op jit(solution)/shard_map/cond/branch_1_fun/and | solution.py:85
  215.0 28.2 %fusion = (f32[4,512]{1,0:T(4,128)S(1)}, f32[4,512,8192]{2,1,0:T(8,128)}) fusion(pred[512,8192]{1,0:T(8,128)(4,1)} %compare_and_fusion, bf16[512,4,96]{0,2,1:T(8,128)(2,1)S(1)} %get-tuple-element.26, bf16[8192,4,96]{0,2,1:T(8,128)(2,1)} %get-tuple-element.27), kind=kOutput, calls=%fused_computation.3 | convolution fusion | flops 3271555072 | bytes 77996032 | tf_op jit(solution)/shard_map/cond/branch_1_fun/qhd,khd->hqk/dot_general | solution.py:81
  243.2 28.1 %fusion.3 = f32[4,512,96]{1,2,0:T(8,128)S(1)} fusion(bf16[8192,4,96]{0,2,1:T(8,128)(2,1)} %get-tuple-element.28, f32[4,512,8192]{2,1,0:T(8,128)} %get-tuple-element.38, f32[4,512]{1,0:T(4,128)S(1)} %broadcast_maximum_fusion, pred[512,8192]{1,0:T(8,128)(4,1)} %compare_and_fusion), kind=kOutput, calls=%fused_computation.6 | convolution fusion | flops 3288334336 | bytes 78389248 | tf_op jit(solution)/shard_map/cond/branch_1_fun/hqk,khd->hqd/dot_general | solution.py:93
  271.3 22.7 %fusion.2 = f32[4,512]{1,0:T(4,128)S(1)} fusion(f32[4,512,8192]{2,1,0:T(8,128)} %get-tuple-element.38, f32[4,512]{1,0:T(4,128)S(1)} %broadcast_maximum_fusion, pred[512,8192]{1,0:T(8,128)(4,1)} %compare_and_fusion), kind=kLoop, calls=%fused_computation.5 | loop fusion | flops 67106816 | bytes 71319552 | tf_op jit(solution)/shard_map/cond/branch_1_fun/reduce_sum | solution.py:92
  294.4 7.8 %convolution_convert_fusion = bf16[512,6144]{1,0:T(8,128)(2,1)} fusion(bf16[512,384]{0,1:T(8,128)(2,1)S(1)} %bitcast.34, bf16[384,6144]{1,0:T(8,128)(2,1)} %param.13), kind=kOutput, calls=%fused_computation.20 | convolution fusion | flops 2419064832 | bytes 11403264 | tf_op jit(solution)/shard_map/dot_general | solution.py:104
  302.2 0.3 copy.25
  302.6 0.3 copy.26
  302.9 0.4 convert_element_type.65
  303.3 0.4 convert_element_type.66
  303.9 2.3 scatter_fusion
  306.2 38.9 %reduce-scatter.2.cloned.1.call-done = bf16[512,768]{1,0:T(8,128)(2,1)} async-done(((bf16[512,6144]{1,0:T(8,128)(2,1)}), bf16[512,768]{1,0:T(8,128)(2,1)}) %reduce-scatter.2.cloned.1.call-update) | async-done | bytes 786448 | tf_op jit(solution)/shard_map/reduce_scatter | solution.py:105
  (55 shorter events, 1.8 us)
Async XLA Ops:
  7.2 69.5 %copy-start = (s32[16,16]{1,0:T(8,128)S(1)}, s32[16,16]{1,0:T(8,128)}, u32[]{:S(2)}) copy-start(s32[16,16]{1,0:T(8,128)} %param.16) | copy-start | bytes 3076
  7.2 47.2 %all-gather.6.cloned.1.call-start = ((), (), s32[]{:S(2)}) async-start(), calls=%async_computation.1 | async-start | bytes 7077888 | tf_op jit(solution)/shard_map/all_gather | solution.py:48
  7.9 133.0 %all-gather.8.cloned.1.call-start = ((), (), s32[]{:S(2)}) async-start(), calls=%async_computation.2 | async-start | bytes 6684672 | tf_op jit(solution)/shard_map/all_gather | solution.py:70
  8.0 18.8 %copy-start.7 = (s32[64]{0:T(128)S(1)}, s32[64]{0:T(128)}, u32[]{:S(2)}) copy-start(s32[64]{0:T(128)} %param.14) | copy-start | bytes 772
  8.0 19.2 %copy-start.6 = (s32[512]{0:T(512)S(1)}, s32[512]{0:T(512)}, u32[]{:S(2)}) copy-start(s32[512]{0:T(512)} %param.15) | copy-start | bytes 6148
  26.8 36.0 %copy-start.8 = (f32[6144]{0:T(1024)S(1)}, f32[6144]{0:T(1024)}, u32[]{:S(2)}) copy-start(f32[6144]{0:T(1024)} %param.11) | copy-start | bytes 73732
  54.4 8.4 %copy-start.2 = (bf16[512,6144]{1,0:T(8,128)(2,1)S(1)}, bf16[512,6144]{1,0:T(8,128)(2,1)}, u32[]{:S(2)}) copy-start(bf16[512,6144]{1,0:T(8,128)(2,1)} %all-gather.6.cloned.1.call-done) | copy-start | bytes 18874372
  75.7 133.5 %all-gather.10.cloned.1.call-start = ((), (), s32[]{:S(2)}) async-start(), calls=%async_computation.4 | async-start | bytes 6684672 | tf_op jit(solution)/shard_map/all_gather | solution.py:71
  76.6 268.6 %reduce-scatter.2.cloned.1.call-start = ((), (), s32[]{:S(2)}) async-start(), calls=%async_computation.3 | async-start | bytes 7077888 | tf_op jit(solution)/shard_map/reduce_scatter | solution.py:105
  294.2 8.0 %copy-start.9 = (s32[32]{0:T(128)S(1)}, s32[32]{0:T(128)}, u32[]{:S(2)}) copy-start(s32[32]{0:T(128)} %param.17) | copy-start | bytes 388
  294.2 8.0 %copy-start.3 = (bf16[512,4,96]{0,2,1:T(8,128)(2,1)S(1)}, bf16[512,4,96]{0,2,1:T(8,128)(2,1)}, u32[]{:S(2)}) copy-start(bf16[512,4,96]{0,2,1:T(8,128)(2,1)} %maximum_convert_fusion) | copy-start | bytes 1179652
  294.3 8.3 %copy-start.4 = (bf16[512,1,4,96]{0,3,2,1:T(8,128)(2,1)S(1)}, bf16[512,1,4,96]{0,3,2,1:T(8,128)(2,1)}, u32[]{:S(2)}) copy-start(bf16[512,1,4,96]{0,3,2,1:T(8,128)(2,1)} %slice.58) | copy-start | bytes 1179652
  294.4 50.8 %copy-start.1 = (s32[16,16]{1,0:T(8,128)S(1)}, s32[16,16]{1,0:T(8,128)}, u32[]{:S(2)}) copy-start(s32[16,16]{1,0:T(8,128)} %param.16) | copy-start | bytes 3076
  306.2 38.9 %copy-start.5 = (bf16[2,32,16,384]{3,2,1,0:T(8,128)(2,1)}, bf16[2,32,16,384]{3,2,1,0:T(8,128)(2,1)S(1)}, u32[]{:S(2)}) copy-start(bf16[2,32,16,384]{3,2,1,0:T(8,128)(2,1)S(1)} %scatter_fusion) | copy-start | bytes 2359300
Sparse Core Ops, SparseCore 0:
  9.7 44.6 all-gather.5
  75.8 64.9 all-gather.7
  143.0 66.1 all-gather.9
  302.3 42.7 reduce-scatter.1
where the time goes:
time: 352 us
  waiting for transfers between devices  178 us (51%)
  matrix products  75.9 us (22%)
  other arithmetic  39.4 us (11%)
  local copies, waits for them, and re-layouts  23.8 us (7%)
  blocking collectives  19.2 us (5%)
  between operations  14.7 us (4%)
    all_gather x1, waiting for transfers between devices, per_device(): value_piece = lax.all_gather(values, 'blk', axis=0, tiled=True)  68.3 us
    all_gather x1, waiting for transfers between devices, per_device(): key_piece = lax.all_gather(key_rows, 'blk', axis=0, tiled=True)  43.4 us
    reduce_scatter x1, waiting for transfers between devices, per_device(): lax.psum_scatter(partial_term.astype(jnp.bfloat16), 'tp', scatter_dimensi...  38.9 us
    dot_general x1, matrix products, compute(): jnp.einsum('qhd,khd->hqk', queries, key_piece, preferred_element_type=jnp...  28.2 us
    dot_general x1, matrix products, compute(): jnp.einsum('hqk,khd->hqd', weights.astype(jnp.bfloat16), value_piece, pre...  28.1 us
    all_gather x1, waiting for transfers between devices, per_device(): whole = lax.all_gather(hidden_in, 'tp', axis=1, tiled=True)  26.9 us
    reduce_sum x1, other arithmetic, compute(): totals = jnp.sum(weights, axis=-1)  22.7 us
    all_gather x1, blocking collectives, per_device(): segment_piece = lax.all_gather(segment_ids, 'blk', axis=0, tiled=True)  19.2 us
  transfers between devices with their start and end apart: 4, of which 4 were waited for; matrix products, arithmetic and copies ran while one was open for 7% of the time, Pallas kernels for 0%

commit v1 on v0

--- a/solution.py
+++ b/solution.py
@@ -45,7 +45,9 @@
 
 def per_device(hidden_in, ln_gain, w_qkv, w_out, doc_lengths, segment_ids, pair_table, page_table):
     row_count = hidden_in.shape[0]
-    whole = lax.all_gather(hidden_in, "tp", axis=1, tiled=True)
+    whole = jnp.concatenate(
+        lax.all_to_all(jnp.stack([hidden_in] * lax.axis_size("tp")), "tp", 0, 0), axis=1
+    )
     normed = layer_norm(whole, ln_gain)
     width = whole.shape[1]
     col_count = w_qkv.shape[2]

time: 352 us -> 397 us (1.13)
  waiting for transfers between devices: 178 us -> 203 us
  local copies, waits for them, and re-layouts: 23.8 us -> 36.5 us
  starting transfers between devices: 0.16 us -> 6.89 us
    all_to_all x0 -> x1, waiting for transfers between devices: none -> 51.9 us  [per_device(): lax.all_to_all(jnp.stack([hidden_in] * lax.axis_size('tp')), 'tp', 0, 0)]
    all_gather x1 -> x0, waiting for transfers between devices: 26.9 us -> none  [per_device(): whole = lax.all_gather(hidden_in, 'tp', axis=1, tiled=True)]
    all_to_all x0 -> x1, local copies, waits for them, and re-layouts: none -> 8.65 us  [per_device(): lax.all_to_all(jnp.stack([hidden_in] * lax.axis_size('tp')), 'tp', 0, 0)]
    all_to_all x0 -> x1, starting transfers between devices: none -> 6.8 us  [per_device(): lax.all_to_all(jnp.stack([hidden_in] * lax.axis_size('tp')), 'tp', 0, 0)]
    another operation x1 -> x2, local copies, waits for them, and re-layouts: 0.1 us -> 4.3 us  [the longest x1 4.2 us: per_device(): jnp.stack([hidden_in] * lax.axis_size('tp'))]
  transfers between devices with their start and end apart: 4 -> 4, of which waited for: 4 -> 4; matrix products, arithmetic and copies ran while one was open for 7% -> 6% of each run, Pallas kernels for 0% -> 0%
where the time goes in v1:
time: 397 us; the launch traced here: 396 us
  waiting for transfers between devices  203 us (51%)
  matrix products  74.3 us (19%)
  other arithmetic  41.3 us (10%)
  local copies, waits for them, and re-layouts  36.5 us (9%)
  blocking collectives  19.5 us (5%)
  between operations  14.7 us (4%)
  starting transfers between devices  6.89 us (2%)
    all_gather x1, waiting for transfers between devices, per_device(): value_piece = lax.all_gather(values, 'blk', axis=0, tiled=True)  68.3 us
    all_to_all x1, waiting for transfers between devices, per_device(): lax.all_to_all(jnp.stack([hidden_in] * lax.axis_size('tp')), 'tp', 0, 0)  51.9 us
    all_gather x1, waiting for transfers between devices, per_device(): key_piece = lax.all_gather(key_rows, 'blk', axis=0, tiled=True)  43.4 us
    reduce_scatter x1, waiting for transfers between devices, per_device(): lax.psum_scatter(partial_term.astype(jnp.bfloat16), 'tp', scatter_dimensi...  38.9 us
    dot_general x1, matrix products, compute(): jnp.einsum('qhd,khd->hqk', queries, key_piece, preferred_element_type=jnp...  28.2 us
    dot_general x1, matrix products, compute(): jnp.einsum('hqk,khd->hqd', weights.astype(jnp.bfloat16), value_piece, pre...  28.1 us
    reduce_sum x1, other arithmetic, compute(): totals = jnp.sum(weights, axis=-1)  22.7 us
    all_gather x1, blocking collectives, per_device(): segment_piece = lax.all_gather(segment_ids, 'blk', axis=0, tiled=True)  19.5 us
  transfers between devices with their start and end apart: 4, of which 4 were waited for; matrix products, arithmetic and copies ran while one was open for 6% of the time, Pallas kernels for 0%

profile of v1, /device:TPU:1, one launch (start us, length us, event | category | flops | bytes accessed | tf_op | source)
XLA Modules:
  0.0 396.0 jit_solution(484392015133474613)
XLA Ops:
  7.2 4.2 %stack.4 = bf16[8,512,768]{2,1,0:T(8,128)(2,1)} broadcast(bf16[512,768]{1,0:T(8,128)(2,1)} %param.10), dimensions={1,2} | broadcast | bytes 7077888 | tf_op jit(solution)/shard_map/stack | solution.py:49
  11.4 6.8 %all-to-all-start = ((bf16[8,512,768]{2,1,0:T(8,128)(2,1)}), bf16[8,512,768]{2,1,0:T(8,128)(2,1)}, u32[]{:S(2)}, u32[]{:S(2)}) async-start(bf16[8,512,768]{2,1,0:T(8,128)(2,1)} %stack.4), calls=%async_computation | async-start | bytes 12582912 | tf_op jit(solution)/shard_map/all_to_all | solution.py:49
  18.2 18.6 %copy.31 = bf16[6144,3,384]{0,2,1:T(8,128)(2,1)} copy(bf16[6144,3,384]{2,0,1:T(8,128)(2,1)} %param.12) | data formatting | bytes 28311552 | tf_op args[2]
  37.5 51.9 %all-to-all-done = bf16[8,512,768]{2,1,0:T(8,128)(2,1)} async-done(((bf16[8,512,768]{2,1,0:T(8,128)(2,1)}), bf16[8,512,768]{2,1,0:T(8,128)(2,1)}, u32[]{:S(2)}, u32[]{:S(2)}) %all-to-all-start) | async-done | bytes 6291488 | tf_op jit(solution)/shard_map/all_to_all | solution.py:49
  89.4 8.7 %copy.30 = bf16[8,512,768]{1,2,0:T(8,128)(2,1)} copy(bf16[8,512,768]{2,1,0:T(8,128)(2,1)} %all-to-all-done) | data formatting | bytes 12582912 | tf_op jit(solution)/shard_map/all_to_all | solution.py:49
  98.1 3.8 convert_reduce_fusion
  101.9 4.5 %fusion.10 = f32[512]{0:T(512)S(1)} fusion(bf16[8,512,768]{1,2,0:T(8,128)(2,1)} %copy.30, f32[512]{0:T(512)S(1)} %broadcast_multiply_fusion), kind=kLoop, calls=%fused_computation.17 | loop fusion | flops 12582400 | bytes 6295552 | tf_op jit(solution)/shard_map/reduce_sum | solution.py:16
  106.4 2.0 fusion.12
  108.4 10.3 %fusion.17 = f32[512,3,4,96]{0,3,2,1:T(8,128)S(1)} fusion(bf16[512,6144,1,1]{0,1,3,2:T(8,128)(2,1)S(1)} %bitcast.35, bf16[3,4,96,6144]{3,2,1,0:T(8,128)(2,1)} %bitcast.34), kind=kOutput, calls=%fused_computation.54 | convolution fusion | flops 7247757312 | bytes 22806528 | tf_op jit(solution)/shard_map/dot_general | solution.py:55
  118.9 0.8 maximum_convert_fusion
  119.8 0.8 slice.58
  120.9 0.6 fusion.16
  122.2 19.5 %all-gather.1 = s32[16,1,512]{2,1,0:T(1,128)S(1)} all-gather(s32[1,1,512]{2,1,0:T(1,128)S(1)} %bitcast.38), channel_id=1, replica_groups=mesh['blk'=16,'tp'=8] {'blk'}, dimensions={0}, use_global_device_ids=true | all-gather | bytes 34816 | tf_op jit(solution)/shard_map/all_gather | solution.py:74
  141.8 43.4 %all-gather.5.cloned.1.call-done = bf16[8192,4,96]{0,2,1:T(8,128)(2,1)} async-done(((bf16[512,4,96]{0,2,1:T(8,128)(2,1)}), bf16[8192,4,96]{0,2,1:T(8,128)(2,1)}) %all-gather.5.cloned.1.call-update) | async-done | bytes 6291472 | tf_op jit(solution)/shard_map/all_gather | solution.py:72
  185.2 68.3 %all-gather.7.cloned.1.call-done = bf16[8192,1,4,96]{0,3,2,1:T(8,128)(2,1)} async-done(((bf16[512,1,4,96]{0,3,2,1:T(8,128)(2,1)}), bf16[8192,1,4,96]{0,3,2,1:T(8,128)(2,1)}) %all-gather.7.cloned.1.call-update) | async-done | bytes 6291472 | tf_op jit(solution)/shard_map/all_gather | solution.py:73
  253.5 85.0 %conditional.1 = (f32[4,512]{1,0:T(4,128)S(1)}, f32[4,512,96]{1,2,0:T(8,128)S(1)}) conditional(s32[]{:T(128)} %convert_element_type.61, () %tuple.16, (pred[8192]{0:T(1024)(128)(4,1)S(1)}, s32[512]{0:T(512)S(1)}, s32[8192]{0:T(1024)S(1)}, s32[8192]{0:T(1024)S(1)}, s32[]{:T(128)}, /*index=5*/s32[512]{0:T(512)S(1)}, bf16[512,4,96]{0,2,1:T(8,128)(2,1)S(1)}, ...), branch_computations={%region_6.7_spmd, %region_7.10_spmd} | conditional | flops 6643776000 | bytes 231997456 | solution.py:103
  253.5 5.8 %compare_and_fusion = pred[512,8192]{1,0:T(8,128)(4,1)} fusion(s32[8192]{0:T(1024)S(1)} %get-tuple-element.23, s32[8192]{0:T(1024)S(1)} %get-tuple-element.22, s32[512]{0:T(512)S(1)} %broadcast_add_fusion, s32[512]{0:T(512)S(1)} %get-tuple-element.21, pred[8192]{0:T(1024)(128)(4,1)S(1)} %get-tuple-element.20), kind=kLoop, calls=%fused_computation.8 | loop fusion | flops 16777216 | bytes 4272128 | tf_op jit(solution)/shard_map/cond/branch_1_fun/and | solution.py:87
  259.3 28.2 %fusion = (f32[4,512]{1,0:T(4,128)S(1)}, f32[4,512,8192]{2,1,0:T(8,128)}) fusion(pred[512,8192]{1,0:T(8,128)(4,1)} %compare_and_fusion, bf16[512,4,96]{0,2,1:T(8,128)(2,1)S(1)} %get-tuple-element.26, bf16[8192,4,96]{0,2,1:T(8,128)(2,1)} %get-tuple-element.27), kind=kOutput, calls=%fused_computation.3 | convolution fusion | flops 3271555072 | bytes 77996032 | tf_op jit(solution)/shard_map/cond/branch_1_fun/qhd,khd->hqk/dot_general | solution.py:83
  287.5 28.1 %fusion.3 = f32[4,512,96]{1,2,0:T(8,128)S(1)} fusion(bf16[8192,4,96]{0,2,1:T(8,128)(2,1)} %get-tuple-element.28, f32[4,512,8192]{2,1,0:T(8,128)} %get-tuple-element.38, f32[4,512]{1,0:T(4,128)S(1)} %broadcast_maximum_fusion, pred[512,8192]{1,0:T(8,128)(4,1)} %compare_and_fusion), kind=kOutput, calls=%fused_computation.6 | convolution fusion | flops 3288334336 | bytes 78389248 | tf_op jit(solution)/shard_map/cond/branch_1_fun/hqk,khd->hqd/dot_general | solution.py:95
  315.6 22.7 %fusion.2 = f32[4,512]{1,0:T(4,128)S(1)} fusion(f32[4,512,8192]{2,1,0:T(8,128)} %get-tuple-element.38, f32[4,512]{1,0:T(4,128)S(1)} %broadcast_maximum_fusion, pred[512,8192]{1,0:T(8,128)(4,1)} %compare_and_fusion), kind=kLoop, calls=%fused_computation.5 | loop fusion | flops 67106816 | bytes 71319552 | tf_op jit(solution)/shard_map/cond/branch_1_fun/reduce_sum | solution.py:94
  338.7 7.8 %convolution_convert_fusion = bf16[512,6144]{1,0:T(8,128)(2,1)} fusion(bf16[512,384]{0,1:T(8,128)(2,1)S(1)} %bitcast.36, bf16[384,6144]{1,0:T(8,128)(2,1)} %param.13), kind=kOutput, calls=%fused_computation.20 | convolution fusion | flops 2419064832 | bytes 11403264 | tf_op jit(solution)/shard_map/dot_general | solution.py:106
  347.5 0.4 convert_element_type.71
  348.2 2.3 scatter_fusion
  350.5 38.9 %reduce-scatter.2.cloned.1.call-done = bf16[512,768]{1,0:T(8,128)(2,1)} async-done(((bf16[512,6144]{1,0:T(8,128)(2,1)}), bf16[512,768]{1,0:T(8,128)(2,1)}) %reduce-scatter.2.cloned.1.call-update) | async-done | bytes 786448 | tf_op jit(solution)/shard_map/reduce_scatter | solution.py:107
  (58 shorter events, 2.7 us)
Async XLA Ops:
  7.2 113.5 %copy-start = (s32[16,16]{1,0:T(8,128)S(1)}, s32[16,16]{1,0:T(8,128)}, u32[]{:S(2)}) copy-start(s32[16,16]{1,0:T(8,128)} %param.16) | copy-start | bytes 3076
  7.2 11.0 %copy-start.6 = (f32[6144]{0:T(1024)S(1)}, f32[6144]{0:T(1024)}, u32[]{:S(2)}) copy-start(f32[6144]{0:T(1024)} %param.11) | copy-start | bytes 73732
  11.4 78.1 %all-to-all-start = ((bf16[8,512,768]{2,1,0:T(8,128)(2,1)}), bf16[8,512,768]{2,1,0:T(8,128)(2,1)}, u32[]{:S(2)}, u32[]{:S(2)}) async-start(bf16[8,512,768]{2,1,0:T(8,128)(2,1)} %stack.4), calls=%async_computation | async-start | bytes 12582912 | tf_op jit(solution)/shard_map/all_to_all | solution.py:49
  18.2 167.0 %all-gather.5.cloned.1.call-start = ((), (), s32[]{:S(2)}) async-start(), calls=%async_computation.2 | async-start | bytes 6684672 | tf_op jit(solution)/shard_map/all_gather | solution.py:72
  18.2 18.6 %copy-start.8 = (s32[64]{0:T(128)S(1)}, s32[64]{0:T(128)}, u32[]{:S(2)}) copy-start(s32[64]{0:T(128)} %param.14) | copy-start | bytes 772
  18.2 19.0 %copy-start.7 = (s32[512]{0:T(512)S(1)}, s32[512]{0:T(512)}, u32[]{:S(2)}) copy-start(s32[512]{0:T(512)} %param.15) | copy-start | bytes 6148
  98.1 8.3 %copy-start.2 = (bf16[8,512,768]{1,2,0:T(8,128)(2,1)S(1)}, bf16[8,512,768]{1,2,0:T(8,128)(2,1)}, u32[]{:S(2)}) copy-start(bf16[8,512,768]{1,2,0:T(8,128)(2,1)} %copy.30) | copy-start | bytes 18874372
  119.8 133.7 %all-gather.7.cloned.1.call-start = ((), (), s32[]{:S(2)}) async-start(), calls=%async_computation.4 | async-start | bytes 6684672 | tf_op jit(solution)/shard_map/all_gather | solution.py:73
  120.6 268.8 %reduce-scatter.2.cloned.1.call-start = ((), (), s32[]{:S(2)}) async-start(), calls=%async_computation.3 | async-start | bytes 7077888 | tf_op jit(solution)/shard_map/reduce_scatter | solution.py:107
  338.5 8.0 %copy-start.9 = (s32[32]{0:T(128)S(1)}, s32[32]{0:T(128)}, u32[]{:S(2)}) copy-start(s32[32]{0:T(128)} %param.17) | copy-start | bytes 388
  338.5 8.0 %copy-start.3 = (bf16[512,4,96]{0,2,1:T(8,128)(2,1)S(1)}, bf16[512,4,96]{0,2,1:T(8,128)(2,1)}, u32[]{:S(2)}) copy-start(bf16[512,4,96]{0,2,1:T(8,128)(2,1)} %maximum_convert_fusion) | copy-start | bytes 1179652
  338.5 8.3 %copy-start.4 = (bf16[512,1,4,96]{0,3,2,1:T(8,128)(2,1)S(1)}, bf16[512,1,4,96]{0,3,2,1:T(8,128)(2,1)}, u32[]{:S(2)}) copy-start(bf16[512,1,4,96]{0,3,2,1:T(8,128)(2,1)} %slice.58) | copy-start | bytes 1179652
  338.6 50.8 %copy-start.1 = (s32[16,16]{1,0:T(8,128)S(1)}, s32[16,16]{1,0:T(8,128)}, u32[]{:S(2)}) copy-start(s32[16,16]{1,0:T(8,128)} %param.16) | copy-start | bytes 3076
  350.5 38.9 %copy-start.5 = (bf16[2,32,16,384]{3,2,1,0:T(8,128)(2,1)}, bf16[2,32,16,384]{3,2,1,0:T(8,128)(2,1)S(1)}, u32[]{:S(2)}) copy-start(bf16[2,32,16,384]{3,2,1,0:T(8,128)(2,1)S(1)} %scatter_fusion) | copy-start | bytes 2359300
Sparse Core Ops, SparseCore 0:
  119.9 65.2 all-gather.4
  187.3 66.1 all-gather.6
  346.6 42.7 reduce-scatter.1
